TPU v7x, 32 devices: a whole 2x2x4 slice. The times are simulated.
32 devices in a mesh: groups: 2 (over y), patch: 8 (over z, x), heads: 2 (over core).
Axes of the slice: x: 2, y: 2, z: 4, core: 2. Of those that a mesh axis runs over, the one named last changes fastest.
Arguments:
- hidden_in: bfloat16 [512, 1280], P(('groups', 'patch'), 'heads'), parts along dimension 0, may hold values from -150 to 150
- gn_gain: float32 [1280], P('heads'), may hold values from 0.25 to 1.75
- gn_bias: float32 [1280], P('heads'), may hold values from -3 to 3
- w_in: bfloat16 [1280, 1280], P(None, 'heads'), may hold values from -0.15625 to 0.15625
- b_in: float32 [1280], P('heads'), may hold values from -3 to 3
- ln_gain: float32 [1280], replicated, may hold values from 0.25 to 1.75
- ln_bias: float32 [1280], replicated, may hold values from -3 to 3
- w_qkv: bfloat16 [3, 1280, 1280], P(None, None, 'heads'), may hold values from -0.15625 to 0.15625
- stale_kv: bfloat16 [2, 512, 1280], P(None, ('groups', 'patch'), 'heads'), parts along dimension 1, may hold values from -64 to 64
- w_out: bfloat16 [1280, 1280], P('heads'), may hold values from -0.15625 to 0.15625
- b_out: float32 [1280], P('heads'), may hold values from -3 to 3
Outputs:
- hidden_out: float32 [512, 1280], P(('groups', 'patch'), 'heads'), parts along dimension 0
There are 2 independent parts, one for each index of `groups`. A program takes and returns all parts, laid end to end along the dimension named above; an argument that names none is the same for every part. Nothing has to cross between parts.
All inputs are finite; a program needn't handle non-finite values.
Results may differ from a plain program's by a relative error of at most 0.035.
Values may be sent and summed in bfloat16 or wider, within the bound.
No kernel may reach another device: no remote copies, remote signals or barrier semaphores. Data moves between devices by JAX's collectives and lax.ppermute only.
A program may use at most 128 MiB of HBM per device.

v0:
```python
import functools

import jax
import jax.numpy as jnp
from jax import lax
from jax.experimental import pallas as pl
from jax.experimental.pallas import tpu as pltpu
from jax.sharding import PartitionSpec as P


HD = 64
GROUPS = 32
STAT_ROWS = 4
COVER = 10_000_000_000
VMEM = pltpu.VMEM
BF = jnp.bfloat16
F32 = jnp.float32


def call(kernel, out_shape, n_in, scratch=(), spaces=None, flops=0, extra=0):
    return pl.pallas_call(
        kernel,
        out_shape=out_shape,
        in_specs=[pl.BlockSpec(memory_space=(spaces or {}).get(i, VMEM)) for i in range(n_in)],
        out_specs=jax.tree.map(lambda _: pl.BlockSpec(memory_space=VMEM), out_shape),
        scratch_shapes=list(scratch),
        cost_estimate=pl.CostEstimate(flops=flops, bytes_accessed=1 << 17, transcendentals=0),
        compiler_params=pltpu.CompilerParams(vmem_limit_bytes=(8 << 20) + extra),
    )


def sds(shape, dtype):
    return jax.ShapeDtypeStruct(shape, dtype)


def col_stats(x):
    mean = jnp.mean(x, axis=0, keepdims=True)
    cen = x - mean
    return mean, jnp.sum(cen * cen, axis=0, keepdims=True)


def tick_kernel(out_ref):
    out_ref[...] = jnp.zeros_like(out_ref)


def stats_kernel(own_ref, other_ref, gain_ref, bias_ref, b_in_ref, tick_ref, stat_ref, gb_ref):
    _, width = own_ref.shape
    rows = []
    for ref in (own_ref, other_ref):
        mean, m2 = col_stats(ref[...].astype(F32))
        rows += [mean, m2]
    stat_ref[...] = jnp.concatenate(rows, axis=0)
    gb_ref[0:1, :] = gain_ref[...].reshape(1, width)
    gb_ref[1:2, :] = bias_ref[...].reshape(1, width)
    gb_ref[2:3, :] = b_in_ref[...].reshape(1, width)


def merge_stats(parts, count):
    mean = parts[0][0]
    for p in parts[1:]:
        mean = mean + p[0]
    mean = mean * (1.0 / len(parts))
    m2 = None
    for p in parts:
        dev = p[0] - mean
        term = p[1] + count * (dev * dev)
        m2 = term if m2 is None else m2 + term
    return mean, m2


def half_stats(refs, half, count):
    at = 2 * half
    rows = [r[...] for r in refs]
    return merge_stats([(r[at : at + 1], r[at + 1 : at + 2]) for r in rows], count)


def merge_kernel(count, *refs):
    out = [row for half in (0, 1) for row in half_stats(refs[:-1], half, count)]
    refs[-1][...] = jnp.concatenate(out, axis=0)


def stack_kernel(*refs):
    rows = refs[0].shape[0]
    for i, r in enumerate(refs[:-1]):
        refs[-1][i * rows : (i + 1) * rows, :] = r[...]


def front_kernel(count, group_size, n_stat, *refs):
    stats, rest = refs[:n_stat], refs[n_stat:]
    own_ref, other_ref, gb_ref, gb2_ref, w_own_ref, w_other_ref, gain_ref, bias_ref, w_ref, stream_ref, out_ref = rest
    _, width = own_ref.shape
    full = 2 * width
    n_groups = width // group_size
    total = count * n_stat
    chan = lax.broadcasted_iota(jnp.int32, (n_groups, width), 1)
    grp = lax.broadcasted_iota(jnp.int32, (n_groups, width), 0) * group_size
    hot = jnp.where((chan >= grp) & (chan < grp + group_size), 1.0, 0.0)

    def over_group(row):
        per = jnp.sum(hot * row, axis=1, keepdims=True)
        return jnp.sum(hot * per, axis=0, keepdims=True)

    low = lax.axis_index("heads") == 0

    def in_order(own, other):
        return jnp.concatenate([jnp.where(low, own, other), jnp.where(low, other, own)], axis=1)

    normed = []
    for half, (x_ref, g_ref) in enumerate(((own_ref, gb_ref), (other_ref, gb2_ref))):
        mean, m2 = half_stats(stats, half, count)
        g_mean = over_group(mean) * (1.0 / group_size)
        dev = mean - g_mean
        var = over_group(m2 + total * (dev * dev)) * (1.0 / (total * group_size))
        scale = lax.rsqrt(var + 1e-06) * g_ref[0:1, :]
        normed.append((x_ref[...].astype(F32) - g_mean) * scale + g_ref[1:2, :])
    normed = in_order(*normed).astype(BF)
    x = []
    for wt_ref, g_ref in ((w_own_ref, gb_ref), (w_other_ref, gb2_ref)):
        x.append((jnp.dot(normed, wt_ref[...], preferred_element_type=F32) + g_ref[2:3, :]).astype(BF))
    stream_ref[...] = x[0]
    x = in_order(*[v.astype(F32) for v in x])
    x = x - jnp.sum(x, axis=1, keepdims=True) / full
    rstd = lax.rsqrt(jnp.sum(x * x, axis=1, keepdims=True) / full + 1e-05)
    row = (x * rstd * gain_ref[...].reshape(1, full) + bias_ref[...].reshape(1, full)).astype(BF)
    for i in range(3):
        out_ref[i] = jnp.dot(row, w_ref[i], preferred_element_type=F32).astype(BF)


def attn_kernel(sources, qkv_ref, *refs):
    n_src = max(s[0] for s in sources) + 1
    srcs, (w_ref, att_ref, send_ref) = refs[:n_src], refs[n_src:]
    tok, width = qkv_ref.shape[1:]

    def rows_of(which, c):
        parts = [qkv_ref[1 + which, :, c]] if sources[0][4] else []
        parts += [srcs[s[0]][s[1 + which] : s[1 + which] + s[3], c] for s in sources]
        return parts[0] if len(parts) == 1 else jnp.concatenate(parts, axis=0)

    pair = 2 * HD
    keys = sum(s[3] for s in sources) + (tok if sources[0][4] else 0)
    low = lax.broadcasted_iota(jnp.int32, (tok, pair), 1) < HD
    ones = jnp.ones((keys, pair), BF)
    cols = [slice(p * pair, (p + 1) * pair) for p in range(width // pair)]
    scores = []
    for c in cols:
        q = qkv_ref[0, :, c].astype(F32) * (HD ** (-0.5))
        q2 = jnp.concatenate([jnp.where(low, q, 0.0), jnp.where(low, 0.0, q)], axis=0).astype(BF)
        scores.append(lax.dot_general(q2, rows_of(0, c), (((1,), (1,)), ((), ())), preferred_element_type=F32))
    tops = [jnp.max(s, axis=1, keepdims=True) for s in scores]
    wts = [jnp.exp(s - m).astype(BF) for s, m in zip(scores, tops)]
    att = []
    for c, w in zip(cols, wts):
        both = jnp.dot(w, jnp.concatenate([rows_of(1, c), ones], axis=1), preferred_element_type=F32)
        out = both[:, :pair] / both[:, pair:]
        att.append(jnp.where(low, out[0:tok], out[tok:]).astype(BF))
    att = jnp.concatenate(att, axis=1)
    att_ref[...] = att
    first = pl.multiple_of((1 - lax.axis_index("heads")) * width, 128)
    send_ref[...] = jnp.dot(att, w_ref[:, pl.ds(first, width)], preferred_element_type=F32)


def own_kernel(att_ref, stream_ref, b_ref, w_ref, out_ref):
    width = stream_ref.shape[1]
    first = pl.multiple_of(lax.axis_index("heads") * width, 128)
    part = jnp.dot(att_ref[...], w_ref[:, pl.ds(first, width)], preferred_element_type=F32)
    out_ref[...] = part + stream_ref[...].astype(F32) + b_ref[...].reshape(1, width)


def body(hidden_in, gn_gain, gn_bias, w_in, b_in, ln_gain, ln_bias, w_qkv, stale_kv, w_out, b_out):
    tok, width = hidden_in.shape
    full = ln_gain.shape[0]
    group_size = full // GROUPS
    n = lax.axis_size("patch")
    swap = [(0, 1), (1, 0)]

    kv_own = stale_kv.reshape(2 * tok, width)
    partner = lambda k: [(i, i ^ k) for i in range(n)]

    def move(x, k):
        return lax.ppermute(x, "patch", partner(k)) if k else lax.ppermute(x, "heads", swap)

    direct = n == 8
    other = move(hidden_in, 0)
    tick = call(tick_kernel, sds((8, 128), F32), 0, flops=COVER)()
    stat_out = sds((STAT_ROWS, width), F32)
    local, gb = call(stats_kernel, (stat_out, sds((3, width), F32)), 6, flops=COVER)(
        hidden_in, other, gn_gain, gn_bias, b_in, tick
    )
    if direct:
        z2, z1 = move(kv_own, 4), move(kv_own, 2)
        z3 = move(kv_own, 6)
        strip_x = move(kv_own, 1)
        gb_other = move(gb, 0)
        w_other = move(w_in, 0)
        m0 = call(functools.partial(merge_kernel, float(1 * tok)), stat_out, 2, flops=COVER)(local, move(local, 1))
        m1 = call(functools.partial(merge_kernel, float(2 * tok)), stat_out, 2, flops=COVER)(m0, move(m0, 4))
        stats = [m1, move(m1, 2)]
        n0 = call(stack_kernel, sds((4 * tok, width), BF), 2)(z2, z1)
        f0 = move(n0, 1)
        f1 = move(z3, 1)
        strips = [strip_x, n0, f0, z3, f1]
        sources = [(0, 0, tok, tok, True), (1, 0 * tok, 1 * tok, tok, True), (1, 2 * tok, 3 * tok, tok, True), (2, 0 * tok, 1 * tok, tok, True), (2, 2 * tok, 3 * tok, tok, True), (3, 0, tok, tok, True), (4, 0, tok, tok, True)]
    else:
        gb_other = move(gb, 0)
        w_other = move(w_in, 0)
        rows = lax.all_gather(local, "patch")
        stats = [rows[i] for i in range(n)]

    count = float(tok * n) / len(stats)
    stream, qkv = call(
        functools.partial(front_kernel, count, group_size, len(stats)),
        (sds((tok, width), BF), sds((3, tok, width), BF)),
        len(stats) + 9,
        flops=COVER,
    )(*stats, hidden_in, other, gb, gb_other, w_in, w_other, ln_gain, ln_bias, w_qkv)
    n_keys = n * tok
    if not direct:
        kv_all = lax.all_gather(stale_kv, "patch", axis=1, tiled=True)
        kv_all = lax.dynamic_update_slice(kv_all, qkv[1:], (0, lax.axis_index("patch") * tok, 0))
        strips = [kv_all.reshape(2 * n_keys, width)]
        sources = [(0, 0, n_keys, n_keys, False)]
    attended, send = call(
        functools.partial(attn_kernel, sources),
        (sds((tok, width), BF), sds((tok, width), F32)),
        2 + len(strips),
        extra=64 * tok * n_keys + 4 * n_keys * width,
    )(qkv, *strips, w_out)
    received = move(send, 0)
    mine = call(own_kernel, sds((tok, width), F32), 4)(attended, stream, b_out, w_out)
    return mine + received


def solution(mesh):
    placed = (
        P(("groups", "patch"), "heads"),
        P("heads"),
        P("heads"),
        P(None, "heads"),
        P("heads"),
        P(),
        P(),
        P(None, None, "heads"),
        P(None, ("groups", "patch"), "heads"),
        P("heads", None),
        P("heads"),
    )

    return jax.shard_map(body, mesh=mesh, in_specs=placed, out_specs=P(("groups", "patch"), "heads"), check_vma=False)
```

profile of v0, /device:TPU:0, one launch (start us, length us, event | category | flops | bytes accessed | tf_op | source)
XLA Modules:
  0.0 30.0 jit_solution(9939197861381710211)
XLA Ops:
  0.0 0.0 copy-start.3
  0.0 0.6 %collective-permute-start = (bf16[32,640]{1,0:T(8,128)(2,1)}, bf16[32,640]{1,0:T(8,128)(2,1)S(1)}, u32[]{:S(2)}, u32[]{:S(2)}) collective-permute-start(bf16[32,640]{1,0:T(8,128)(2,1)} %refs_2_.1), channel_id=1, source_target_pairs={{0,1},{1,0},{2,3},{3,2},{4,5},{5,4},{6,7},{7,6},{8,9},{9,8},{10,11... | collective-permute-start | bytes 122888 | tf_op jit(solution)/shard_map/ppermute | solution.py:180
  0.6 1.1 %collective-permute-done.other_ref.refs_3_ = bf16[32,640]{1,0:T(8,128)(2,1)S(1)} collective-permute-done((bf16[32,640]{1,0:T(8,128)(2,1)}, bf16[32,640]{1,0:T(8,128)(2,1)S(1)}, u32[]{:S(2)}, u32[]{:S(2)}) %collective-permute-start) | collective-permute-done | bytes 40992 | tf_op jit(solution)/shard_map/ppermute | solution.py:180
  1.7 0.0 copy-done.3
  1.7 0.0 copy-done.6
  1.7 0.0 copy-done.7
  1.7 0.0 copy-done.8
  1.7 0.1 shard_map.110
  1.7 0.0 copy-start.9
  1.8 2.9 %collective-permute-start.1 = (f32[4,640]{1,0:T(4,128)S(1)}, f32[4,640]{1,0:T(4,128)S(1)}, u32[]{:S(2)}, u32[]{:S(2)}) collective-permute-start(f32[4,640]{1,0:T(4,128)S(1)} %get-tuple-element.11.refs_0_), channel_id=1, source_target_pairs={{0,2},{2,0},{4,6},{6,4},{8,10},{10,8},{12,14},{14,12},{1,3},{3,1},... | collective-permute-start | bytes 30728 | tf_op jit(solution)/shard_map/ppermute | solution.py:180
  4.6 0.0 copy-done.2
  4.6 0.0 collective-permute-start.5
  4.7 1.6 %collective-permute-done.1.refs_1_ = f32[4,640]{1,0:T(4,128)S(1)} collective-permute-done((f32[4,640]{1,0:T(4,128)S(1)}, f32[4,640]{1,0:T(4,128)S(1)}, u32[]{:S(2)}, u32[]{:S(2)}) %collective-permute-start.1) | collective-permute-done | bytes 10272 | tf_op jit(solution)/shard_map/ppermute | solution.py:180
  6.3 3.2 %collective-permute-start.2 = (f32[4,640]{1,0:T(4,128)S(1)}, f32[4,640]{1,0:T(4,128)S(1)}, u32[]{:S(2)}, u32[]{:S(2)}) collective-permute-start(f32[4,640]{1,0:T(4,128)S(1)} %shard_map.111.refs_0_), channel_id=1, source_target_pairs={{0,8},{2,10},{4,12},{6,14},{8,0},{10,2},{12,4},{14,6},{1,9},{3,11}... | collective-permute-start | bytes 30728 | tf_op jit(solution)/shard_map/ppermute | solution.py:180
  9.5 0.0 copy-done.9
  9.5 0.0 copy-start.5
  9.5 0.1 collective-permute-start.7
  9.6 1.9 %collective-permute-start.8 = (bf16[64,640]{1,0:T(8,128)(2,1)S(1)}, bf16[64,640]{1,0:T(8,128)(2,1)S(1)}, u32[]{:S(2)}, u32[]{:S(2)}) collective-permute-start(bf16[64,640]{1,0:T(8,128)(2,1)S(1)} %bitcast.4), channel_id=1, source_target_pairs={{0,4},{2,6},{4,0},{6,2},{8,12},{10,14},{12,8},{14,10},{1,5},{3,7},... | collective-permute-start | bytes 245768 | tf_op jit(solution)/shard_map/ppermute | solution.py:180
  11.5 2.5 %collective-permute-start.10 = (bf16[64,640]{1,0:T(8,128)(2,1)S(1)}, bf16[64,640]{1,0:T(8,128)(2,1)S(1)}, u32[]{:S(2)}, u32[]{:S(2)}) collective-permute-start(bf16[64,640]{1,0:T(8,128)(2,1)S(1)} %bitcast.5), channel_id=1, source_target_pairs={{0,12},{2,14},{4,8},{6,10},{8,4},{10,6},{12,0},{14,2},{1,13},{3,15... | collective-permute-start | bytes 245768 | tf_op jit(solution)/shard_map/ppermute | solution.py:180
  14.0 0.0 collective-permute-done.2.refs_1_
  14.0 0.7 %collective-permute-start.3 = (f32[4,640]{1,0:T(4,128)S(1)}, f32[4,640]{1,0:T(4,128)S(1)}, u32[]{:S(2)}, u32[]{:S(2)}) collective-permute-start(f32[4,640]{1,0:T(4,128)S(1)} %shard_map.112.refs_0_), channel_id=1, source_target_pairs={{0,4},{2,6},{4,0},{6,2},{8,12},{10,14},{12,8},{14,10},{1,5},{3,7},... | collective-permute-start | bytes 30728 | tf_op jit(solution)/shard_map/ppermute | solution.py:180
  14.7 2.5 %collective-permute-done.7.refs_0_ = bf16[64,640]{1,0:T(8,128)(2,1)S(1)} collective-permute-done((bf16[64,640]{1,0:T(8,128)(2,1)S(1)}, bf16[64,640]{1,0:T(8,128)(2,1)S(1)}, u32[]{:S(2)}, u32[]{:S(2)}) %collective-permute-start.7) | collective-permute-done | bytes 81952 | tf_op jit(solution)/shard_map/ppermute | solution.py:180
  17.2 0.0 collective-permute-start.4
  17.2 0.0 collective-permute-done.8.refs_1_
  17.2 1.5 %collective-permute-start.6 = (bf16[64,640]{1,0:T(8,128)(2,1)S(1)}, bf16[64,640]{1,0:T(8,128)(2,1)S(1)}, u32[]{:S(2)}, u32[]{:S(2)}) collective-permute-start(bf16[64,640]{1,0:T(8,128)(2,1)S(1)} %bitcast.6), channel_id=1, source_target_pairs={{0,2},{2,0},{4,6},{6,4},{8,10},{10,8},{12,14},{14,12},{1,3},{3,1},... | collective-permute-start | bytes 245768 | tf_op jit(solution)/shard_map/ppermute | solution.py:180
  18.7 0.0 copy-start
  18.7 0.0 collective-permute-done.4.refs_5_
  18.7 1.1 %collective-permute-start.9 = (bf16[128,640]{1,0:T(8,128)(2,1)S(1)}, bf16[128,640]{1,0:T(8,128)(2,1)S(1)}, u32[]{:S(2)}, u32[]{:S(2)}) collective-permute-start(bf16[128,640]{1,0:T(8,128)(2,1)S(1)} %shard_map.114.refs_1_), channel_id=1, source_target_pairs={{0,2},{2,0},{4,6},{6,4},{8,10},{10,8},{12,14},{14,12},{1,3},{3,1},... | collective-permute-start | bytes 491528 | tf_op jit(solution)/shard_map/ppermute | solution.py:180
  19.9 0.0 collective-permute-done.10.refs_3_
  19.9 1.0 %collective-permute-start.11 = (bf16[64,640]{1,0:T(8,128)(2,1)S(1)}, bf16[64,640]{1,0:T(8,128)(2,1)S(1)}, u32[]{:S(2)}, u32[]{:S(2)}) collective-permute-start(bf16[64,640]{1,0:T(8,128)(2,1)S(1)} %collective-permute-done.10.refs_3_), channel_id=1, source_target_pairs={{0,2},{2,0},{4,6},{6,4},{8,10},{10,8},{12,14},{14,12},{1,3},{3,1},... | collective-permute-start | bytes 245768 | tf_op jit(solution)/shard_map/ppermute | solution.py:180
  20.8 0.0 collective-permute-done.3.refs_1_
  20.8 0.0 collective-permute-done.5.refs_7_
  20.9 0.0 slice-done
  20.9 0.0 slice-done.1
  20.9 0.0 copy-done.4
  20.9 0.0 copy-done.5
  20.9 1.8 %shard_map.113 = (bf16[32,640]{1,0:T(8,128)(2,1)S(1)}, bf16[3,32,640]{2,1,0:T(8,128)(2,1)S(1)}) custom-call(f32[4,640]{1,0:T(4,128)S(1)} %shard_map.112.refs_0_, f32[4,640]{1,0:T(4,128)S(1)} %collective-permute-done.3.refs_1_, bf16[32,640]{1,0:T(8,128)(2,1)S(1)} %copy-done.3, bf16[32,640]{1,0:T(8,128)(2,1)S(1)} %collective-permute-done.other_ref.refs_3_, ...), custom_call_target="tpu_custom_call" | custom-call | flops 10000000000 | bytes 131072 | tf_op jit(solution)/shard_map/pallas_call | solution.py:210
  22.7 0.0 copy-start.1
  22.7 0.0 collective-permute-done.6.refs_0_
  22.8 4.6 %collective-permute-done.11.refs_4_ = bf16[64,640]{1,0:T(8,128)(2,1)S(1)} collective-permute-done((bf16[64,640]{1,0:T(8,128)(2,1)S(1)}, bf16[64,640]{1,0:T(8,128)(2,1)S(1)}, u32[]{:S(2)}, u32[]{:S(2)}) %collective-permute-start.11) | collective-permute-done | bytes 81952 | tf_op jit(solution)/shard_map/ppermute | solution.py:180
  27.3 0.0 collective-permute-done.9.refs_2_
  27.3 0.0 copy-done
  27.3 0.6 %shard_map.115 = (bf16[32,640]{1,0:T(8,128)(2,1)S(1)}, f32[32,640]{1,0:T(8,128)S(1)}) custom-call(bf16[3,32,640]{2,1,0:T(8,128)(2,1)S(1)} %get-tuple-element.13.qkv_ref, bf16[64,640]{1,0:T(8,128)(2,1)S(1)} %collective-permute-done.6.refs_0_, bf16[128,640]{1,0:T(8,128)(2,1)S(1)} %shard_map.114.refs_1_, bf16[128,640]{1,0:T(8,128)(2,1)S(1)} %collective-permute-done.9.refs_2_, ...), custom_call_target="tpu_custom_call" | custom-call | bytes 131072 | tf_op jit(solution)/shard_map/pallas_call | solution.py:222
  28.0 0.1 collective-permute-start.12
  28.1 0.0 copy-done.1
  28.1 0.3 shard_map.116
  28.3 1.0 %collective-permute-done.12 = f32[32,640]{1,0:T(8,128)S(1)} collective-permute-done((f32[32,640]{1,0:T(8,128)S(1)}, f32[32,640]{1,0:T(8,128)S(1)}, u32[]{:S(2)}, u32[]{:S(2)}) %collective-permute-start.12) | collective-permute-done | bytes 81952 | tf_op jit(solution)/shard_map/ppermute | solution.py:180
  29.3 0.6 %add.3 = f32[32,640]{1,0:T(8,128)} add(f32[32,640]{1,0:T(8,128)S(1)} %shard_map.116, f32[32,640]{1,0:T(8,128)S(1)} %collective-permute-done.12) | non-fusion elementwise | flops 20480 | bytes 245760 | tf_op jit(solution)/shard_map/add | solution.py:230
  (12 shorter events, 0.1 us)
Async XLA Ops:
  0.0 1.7 %copy-start.3 = (bf16[32,640]{1,0:T(8,128)(2,1)S(1)}, bf16[32,640]{1,0:T(8,128)(2,1)}, u32[]{:S(2)}) copy-start(bf16[32,640]{1,0:T(8,128)(2,1)} %refs_2_.1) | copy-start | bytes 122884
  0.0 1.7 %copy-start.6 = (f32[640]{0:T(1024)S(1)}, f32[640]{0:T(1024)}, u32[]{:S(2)}) copy-start(f32[640]{0:T(1024)} %gain_ref.1) | copy-start | bytes 7684
  0.0 1.7 %copy-start.7 = (f32[640]{0:T(1024)S(1)}, f32[640]{0:T(1024)}, u32[]{:S(2)}) copy-start(f32[640]{0:T(1024)} %bias_ref.1) | copy-start | bytes 7684
  0.0 1.7 %copy-start.8 = (f32[640]{0:T(1024)S(1)}, f32[640]{0:T(1024)}, u32[]{:S(2)}) copy-start(f32[640]{0:T(1024)} %b_in_ref.1) | copy-start | bytes 7684
  0.0 1.6 %collective-permute-start = (bf16[32,640]{1,0:T(8,128)(2,1)}, bf16[32,640]{1,0:T(8,128)(2,1)S(1)}, u32[]{:S(2)}, u32[]{:S(2)}) collective-permute-start(bf16[32,640]{1,0:T(8,128)(2,1)} %refs_2_.1), channel_id=1, source_target_pairs={{0,1},{1,0},{2,3},{3,2},{4,5},{5,4},{6,7},{7,6},{8,9},{9,8},{10,11... | collective-permute-start | bytes 122888 | tf_op jit(solution)/shard_map/ppermute | solution.py:180
  0.6 4.1 %copy-start.2 = (bf16[1280,640]{1,0:T(8,128)(2,1)S(1)}, bf16[1280,640]{1,0:T(8,128)(2,1)}, u32[]{:S(2)}) copy-start(bf16[1280,640]{1,0:T(8,128)(2,1)} %refs_6_.1) | copy-start | bytes 4915204
  1.7 7.8 %copy-start.9 = (bf16[2,32,640]{2,1,0:T(8,128)(2,1)S(1)}, bf16[2,32,640]{2,1,0:T(8,128)(2,1)}, u32[]{:S(2)}) copy-start(bf16[2,32,640]{2,1,0:T(8,128)(2,1)} %param.19) | copy-start | bytes 245764
  1.8 4.5 %collective-permute-start.1 = (f32[4,640]{1,0:T(4,128)S(1)}, f32[4,640]{1,0:T(4,128)S(1)}, u32[]{:S(2)}, u32[]{:S(2)}) collective-permute-start(f32[4,640]{1,0:T(4,128)S(1)} %get-tuple-element.11.refs_0_), channel_id=1, source_target_pairs={{0,2},{2,0},{4,6},{6,4},{8,10},{10,8},{12,14},{14,12},{1,3},{3,1},... | collective-permute-start | bytes 30728 | tf_op jit(solution)/shard_map/ppermute | solution.py:180
  4.6 16.2 %collective-permute-start.5 = (bf16[1280,640]{1,0:T(8,128)(2,1)S(1)}, bf16[1280,640]{1,0:T(8,128)(2,1)S(1)}, u32[]{:S(2)}, u32[]{:S(2)}) collective-permute-start(bf16[1280,640]{1,0:T(8,128)(2,1)S(1)} %copy-done.2), channel_id=1, source_target_pairs={{0,1},{1,0},{2,3},{3,2},{4,5},{5,4},{6,7},{7,6},{8,9},{9,8},{10,11... | collective-permute-start | bytes 4915208 | tf_op jit(solution)/shard_map/ppermute | solution.py:180
  6.3 7.7 %collective-permute-start.2 = (f32[4,640]{1,0:T(4,128)S(1)}, f32[4,640]{1,0:T(4,128)S(1)}, u32[]{:S(2)}, u32[]{:S(2)}) collective-permute-start(f32[4,640]{1,0:T(4,128)S(1)} %shard_map.111.refs_0_), channel_id=1, source_target_pairs={{0,8},{2,10},{4,12},{6,14},{8,0},{10,2},{12,4},{14,6},{1,9},{3,11}... | collective-permute-start | bytes 30728 | tf_op jit(solution)/shard_map/ppermute | solution.py:180
  9.5 11.4 %slice-start = ((s8[4915200]{0:T(1024)(128)(4,1)}), s8[4194304]{0:T(1024)(128)(4,1)S(1)}, s32[]{:S(2)}) async-start(s8[4915200]{0:T(1024)(128)(4,1)} %bitcast.1), calls=%async_computation | async-start | bytes 8388608
  9.5 11.4 %slice-start.1 = ((s8[4915200]{0:T(1024)(128)(4,1)}), s8[720896]{0:T(1024)(128)(4,1)S(1)}, s32[]{:S(2)}) async-start(s8[4915200]{0:T(1024)(128)(4,1)} %bitcast.1), calls=%async_computation.1 | async-start | bytes 1441792
  9.5 11.4 %copy-start.4 = (f32[1280]{0:T(1024)S(1)}, f32[1280]{0:T(1024)}, u32[]{:S(2)}) copy-start(f32[1280]{0:T(1024)} %refs_8_.1) | copy-start | bytes 15364
  9.5 11.4 %copy-start.5 = (f32[1280]{0:T(1024)S(1)}, f32[1280]{0:T(1024)}, u32[]{:S(2)}) copy-start(f32[1280]{0:T(1024)} %refs_9_.1) | copy-start | bytes 15364
  9.5 7.7 %collective-permute-start.7 = (bf16[64,640]{1,0:T(8,128)(2,1)S(1)}, bf16[64,640]{1,0:T(8,128)(2,1)S(1)}, u32[]{:S(2)}, u32[]{:S(2)}) collective-permute-start(bf16[64,640]{1,0:T(8,128)(2,1)S(1)} %bitcast.3), channel_id=1, source_target_pairs={{0,8},{2,10},{4,12},{6,14},{8,0},{10,2},{12,4},{14,6},{1,9},{3,11}... | collective-permute-start | bytes 245768 | tf_op jit(solution)/shard_map/ppermute | solution.py:180
  9.6 7.6 %collective-permute-start.8 = (bf16[64,640]{1,0:T(8,128)(2,1)S(1)}, bf16[64,640]{1,0:T(8,128)(2,1)S(1)}, u32[]{:S(2)}, u32[]{:S(2)}) collective-permute-start(bf16[64,640]{1,0:T(8,128)(2,1)S(1)} %bitcast.4), channel_id=1, source_target_pairs={{0,4},{2,6},{4,0},{6,2},{8,12},{10,14},{12,8},{14,10},{1,5},{3,7},... | collective-permute-start | bytes 245768 | tf_op jit(solution)/shard_map/ppermute | solution.py:180
  11.5 8.4 %collective-permute-start.10 = (bf16[64,640]{1,0:T(8,128)(2,1)S(1)}, bf16[64,640]{1,0:T(8,128)(2,1)S(1)}, u32[]{:S(2)}, u32[]{:S(2)}) collective-permute-start(bf16[64,640]{1,0:T(8,128)(2,1)S(1)} %bitcast.5), channel_id=1, source_target_pairs={{0,12},{2,14},{4,8},{6,10},{8,4},{10,6},{12,0},{14,2},{1,13},{3,15... | collective-permute-start | bytes 245768 | tf_op jit(solution)/shard_map/ppermute | solution.py:180
  14.0 6.8 %collective-permute-start.3 = (f32[4,640]{1,0:T(4,128)S(1)}, f32[4,640]{1,0:T(4,128)S(1)}, u32[]{:S(2)}, u32[]{:S(2)}) collective-permute-start(f32[4,640]{1,0:T(4,128)S(1)} %shard_map.112.refs_0_), channel_id=1, source_target_pairs={{0,4},{2,6},{4,0},{6,2},{8,12},{10,14},{12,8},{14,10},{1,5},{3,7},... | collective-permute-start | bytes 30728 | tf_op jit(solution)/shard_map/ppermute | solution.py:180
  17.2 1.5 %collective-permute-start.4 = (f32[3,640]{1,0:T(4,128)S(1)}, f32[3,640]{1,0:T(4,128)S(1)}, u32[]{:S(2)}, u32[]{:S(2)}) collective-permute-start(f32[3,640]{1,0:T(4,128)S(1)} %get-tuple-element.12.refs_4_), channel_id=1, source_target_pairs={{0,1},{1,0},{2,3},{3,2},{4,5},{5,4},{6,7},{7,6},{8,9},{9,8},{10,11... | collective-permute-start | bytes 23048 | tf_op jit(solution)/shard_map/ppermute | solution.py:180
  17.2 5.5 %collective-permute-start.6 = (bf16[64,640]{1,0:T(8,128)(2,1)S(1)}, bf16[64,640]{1,0:T(8,128)(2,1)S(1)}, u32[]{:S(2)}, u32[]{:S(2)}) collective-permute-start(bf16[64,640]{1,0:T(8,128)(2,1)S(1)} %bitcast.6), channel_id=1, source_target_pairs={{0,2},{2,0},{4,6},{6,4},{8,10},{10,8},{12,14},{14,12},{1,3},{3,1},... | collective-permute-start | bytes 245768 | tf_op jit(solution)/shard_map/ppermute | solution.py:180
  18.7 8.6 %copy-start = (bf16[640,1280]{1,0:T(8,128)(2,1)S(1)}, bf16[640,1280]{1,0:T(8,128)(2,1)}, u32[]{:S(2)}) copy-start(bf16[640,1280]{1,0:T(8,128)(2,1)} %w_ref.1) | copy-start | bytes 4915204
  18.7 8.6 %collective-permute-start.9 = (bf16[128,640]{1,0:T(8,128)(2,1)S(1)}, bf16[128,640]{1,0:T(8,128)(2,1)S(1)}, u32[]{:S(2)}, u32[]{:S(2)}) collective-permute-start(bf16[128,640]{1,0:T(8,128)(2,1)S(1)} %shard_map.114.refs_1_), channel_id=1, source_target_pairs={{0,2},{2,0},{4,6},{6,4},{8,10},{10,8},{12,14},{14,12},{1,3},{3,1},... | collective-permute-start | bytes 491528 | tf_op jit(solution)/shard_map/ppermute | solution.py:180
  19.9 7.5 %collective-permute-start.11 = (bf16[64,640]{1,0:T(8,128)(2,1)S(1)}, bf16[64,640]{1,0:T(8,128)(2,1)S(1)}, u32[]{:S(2)}, u32[]{:S(2)}) collective-permute-start(bf16[64,640]{1,0:T(8,128)(2,1)S(1)} %collective-permute-done.10.refs_3_), channel_id=1, source_target_pairs={{0,2},{2,0},{4,6},{6,4},{8,10},{10,8},{12,14},{14,12},{1,3},{3,1},... | collective-permute-start | bytes 245768 | tf_op jit(solution)/shard_map/ppermute | solution.py:180
  22.7 5.3 %copy-start.1 = (f32[640]{0:T(1024)S(1)}, f32[640]{0:T(1024)}, u32[]{:S(2)}) copy-start(f32[640]{0:T(1024)} %b_ref.1) | copy-start | bytes 7684
  28.0 1.3 %collective-permute-start.12 = (f32[32,640]{1,0:T(8,128)S(1)}, f32[32,640]{1,0:T(8,128)S(1)}, u32[]{:S(2)}, u32[]{:S(2)}) collective-permute-start(f32[32,640]{1,0:T(8,128)S(1)} %get-tuple-element.16), channel_id=1, source_target_pairs={{0,1},{1,0},{2,3},{3,2},{4,5},{5,4},{6,7},{7,6},{8,9},{9,8},{10,11... | collective-permute-start | bytes 245768 | tf_op jit(solution)/shard_map/ppermute | solution.py:180
where the time goes:
time: 30.1 us; the launch traced here: 30 us
  starting transfers between devices  15.5 us (51%)
  waiting for transfers between devices  10.8 us (36%)
  Pallas kernels  2.83 us (9%)
  other arithmetic  0.65 us (2%)
    ppermute x9, starting transfers between devices, move(): lax.ppermute(x, 'patch', partner(k))  14.9 us
    ppermute x9, waiting for transfers between devices, move(): lax.ppermute(x, 'patch', partner(k))  8.72 us
    ppermute x4, waiting for transfers between devices, move(): lax.ppermute(x, 'heads', swap)  2.07 us
    pallas_call x1, Pallas kernels, body(): call(functools.partial(front_kernel, count, group_size, len(stats)), (sds...  1.83 us
    add x1, other arithmetic, body(): return mine + received  0.65 us
    ppermute x4, starting transfers between devices, move(): lax.ppermute(x, 'heads', swap)  0.64 us
    pallas_call x1, Pallas kernels, body(): call(functools.partial(attn_kernel, sources), (sds((tok, width), BF), sds...  0.63 us
  transfers between devices with their start and end apart: 13, of which 5 were waited for; matrix products, arithmetic and copies ran while one was open for 0% of the time, Pallas kernels for 7%

commit v1 on v0

--- a/solution.py
+++ b/solution.py
@@ -85,13 +85,8 @@
         refs[-1][i * rows : (i + 1) * rows, :] = r[...]
 
 
-def front_kernel(count, group_size, n_stat, *refs):
-    stats, rest = refs[:n_stat], refs[n_stat:]
-    own_ref, other_ref, gb_ref, gb2_ref, w_own_ref, w_other_ref, gain_ref, bias_ref, w_ref, stream_ref, out_ref = rest
-    _, width = own_ref.shape
-    full = 2 * width
+def group_sums(width, group_size):
     n_groups = width // group_size
-    total = count * n_stat
     chan = lax.broadcasted_iota(jnp.int32, (n_groups, width), 1)
     grp = lax.broadcasted_iota(jnp.int32, (n_groups, width), 0) * group_size
     hot = jnp.where((chan >= grp) & (chan < grp + group_size), 1.0, 0.0)
@@ -100,20 +95,53 @@
         per = jnp.sum(hot * row, axis=1, keepdims=True)
         return jnp.sum(hot * per, axis=0, keepdims=True)
 
+    return over_group
+
+
+def prep_kernel(count, group_size, stat_ref, own_ref, other_ref, ref_ref, x_ref):
+    width = own_ref.shape[1]
+    over_group = group_sums(width, group_size)
+    out = []
+    for half in (0, 1):
+        mean, m2 = half_stats([stat_ref], half, count)
+        g_mean = over_group(mean) * (1.0 / group_size)
+        dev = mean - g_mean
+        out += [g_mean, over_group(m2 + count * (dev * dev))]
+    ref_ref[...] = jnp.concatenate(out, axis=0)
+    low = lax.axis_index("heads") == 0
+    own, other = own_ref[...].astype(F32), other_ref[...].astype(F32)
+    x_ref[:, :width] = jnp.where(low, own, other)
+    x_ref[:, width:] = jnp.where(low, other, own)
+
+
+def front_kernel(count, group_size, n_stat, *refs):
+    stats, rest = refs[:n_stat], refs[n_stat:]
+    ref_ref, tok_ref, gb_ref, gb2_ref, w_own_ref, w_other_ref, gain_ref, bias_ref, w_ref, stream_ref, out_ref = rest
+    full = tok_ref.shape[1]
+    width = full // 2
+    cells = count * group_size * (n_stat + 1)
+    over_group = group_sums(width, group_size)
     low = lax.axis_index("heads") == 0
 
     def in_order(own, other):
         return jnp.concatenate([jnp.where(low, own, other), jnp.where(low, other, own)], axis=1)
 
-    normed = []
-    for half, (x_ref, g_ref) in enumerate(((own_ref, gb_ref), (other_ref, gb2_ref))):
-        mean, m2 = half_stats(stats, half, count)
-        g_mean = over_group(mean) * (1.0 / group_size)
-        dev = mean - g_mean
-        var = over_group(m2 + total * (dev * dev)) * (1.0 / (total * group_size))
-        scale = lax.rsqrt(var + 1e-06) * g_ref[0:1, :]
-        normed.append((x_ref[...].astype(F32) - g_mean) * scale + g_ref[1:2, :])
-    normed = in_order(*normed).astype(BF)
+    means, scales, shifts = [], [], []
+    for half, g_ref in enumerate((gb_ref, gb2_ref)):
+        at = 2 * half
+        base, spread = ref_ref[at : at + 1, :], ref_ref[at + 1 : at + 2, :]
+        mean_sum = mean_sq = None
+        for s in stats:
+            dev = s[at : at + 1, :] - base
+            term = s[at + 1 : at + 2, :] + count * (dev * dev)
+            mean_sum = dev if mean_sum is None else mean_sum + dev
+            mean_sq = term if mean_sq is None else mean_sq + term
+        off = over_group(mean_sum) * (1.0 / (group_size * (n_stat + 1)))
+        var = (spread + over_group(mean_sq)) * (1.0 / cells) - off * off
+        means.append(base + off)
+        scales.append(lax.rsqrt(jnp.maximum(var, 0.0) + 1e-06) * g_ref[0:1, :])
+        shifts.append(g_ref[1:2, :])
+    normed = ((tok_ref[...] - in_order(*means)) * in_order(*scales) + in_order(*shifts)).astype(BF)
     x = []
     for wt_ref, g_ref in ((w_own_ref, gb_ref), (w_other_ref, gb2_ref)):
         x.append((jnp.dot(normed, wt_ref[...], preferred_element_type=F32) + g_ref[2:3, :]).astype(BF))
@@ -207,12 +235,15 @@
         stats = [rows[i] for i in range(n)]
 
     count = float(tok * n) / len(stats)
+    ref, x_full = call(
+        functools.partial(prep_kernel, count, group_size), (stat_out, sds((tok, full), F32)), 3
+    )(stats[0], hidden_in, other)
     stream, qkv = call(
-        functools.partial(front_kernel, count, group_size, len(stats)),
+        functools.partial(front_kernel, count, group_size, len(stats) - 1),
         (sds((tok, width), BF), sds((3, tok, width), BF)),
-        len(stats) + 9,
+        len(stats) + 8,
         flops=COVER,
-    )(*stats, hidden_in, other, gb, gb_other, w_in, w_other, ln_gain, ln_bias, w_qkv)
+    )(*stats[1:], ref, x_full, gb, gb_other, w_in, w_other, ln_gain, ln_bias, w_qkv)
     n_keys = n * tok
     if not direct:
         kv_all = lax.all_gather(stale_kv, "patch", axis=1, tiled=True)

time: 30.1 us -> 30.4 us (level)
    pallas_call x1 -> x2, Pallas kernels: 1.83 us -> 1.96 us  [the longest x1 1.75 us: body(): call(functools.partial(front_kernel, count, group_size, len(stats) - 1),...]
where the time goes in v1:
time: 30.4 us; the launch traced here: 30.3 us
  starting transfers between devices  15.6 us (51%)
  waiting for transfers between devices  10.9 us (36%)
  Pallas kernels  2.96 us (10%)
  other arithmetic  0.65 us (2%)
    ppermute x9, starting transfers between devices, move(): lax.ppermute(x, 'patch', partner(k))  14.9 us
    ppermute x9, waiting for transfers between devices, move(): lax.ppermute(x, 'patch', partner(k))  8.8 us
    ppermute x4, waiting for transfers between devices, move(): lax.ppermute(x, 'heads', swap)  2.07 us
    pallas_call x1, Pallas kernels, body(): call(functools.partial(front_kernel, count, group_size, len(stats) - 1),...  1.75 us
    add x1, other arithmetic, body(): return mine + received  0.65 us
    ppermute x4, starting transfers between devices, move(): lax.ppermute(x, 'heads', swap)  0.64 us
    pallas_call x1, Pallas kernels, body(): call(functools.partial(attn_kernel, sources), (sds((tok, width), BF), sds...  0.63 us
  transfers between devices with their start and end apart: 13, of which 5 were waited for; matrix products, arithmetic and copies ran while one was open for 0% of the time, Pallas kernels for 7%

profile of v1, /device:TPU:0, one launch (start us, length us, event | category | flops | bytes accessed | tf_op | source)
XLA Modules:
  0.0 30.3 jit_solution(2072869631050867294)
XLA Ops:
  0.0 0.6 %collective-permute-start = (bf16[32,640]{1,0:T(8,128)(2,1)}, bf16[32,640]{1,0:T(8,128)(2,1)S(1)}, u32[]{:S(2)}, u32[]{:S(2)}) collective-permute-start(bf16[32,640]{1,0:T(8,128)(2,1)} %own_ref.3), channel_id=1, source_target_pairs={{0,1},{1,0},{2,3},{3,2},{4,5},{5,4},{6,7},{7,6},{8,9},{9,8},{10,11... | collective-permute-start | bytes 122888 | tf_op jit(solution)/shard_map/ppermute | solution.py:208
  0.6 1.1 %collective-permute-done.other_ref = bf16[32,640]{1,0:T(8,128)(2,1)S(1)} collective-permute-done((bf16[32,640]{1,0:T(8,128)(2,1)}, bf16[32,640]{1,0:T(8,128)(2,1)S(1)}, u32[]{:S(2)}, u32[]{:S(2)}) %collective-permute-start) | collective-permute-done | bytes 40992 | tf_op jit(solution)/shard_map/ppermute | solution.py:208
  1.7 0.0 copy-done.1
  1.7 0.0 copy-done.6
  1.7 0.0 copy-done.7
  1.7 0.0 copy-done.8
  1.7 0.1 shard_map.110
  1.7 0.0 copy-start.9
  1.8 2.9 %collective-permute-start.1 = (f32[4,640]{1,0:T(4,128)S(1)}, f32[4,640]{1,0:T(4,128)S(1)}, u32[]{:S(2)}, u32[]{:S(2)}) collective-permute-start(f32[4,640]{1,0:T(4,128)S(1)} %get-tuple-element.13.refs_0_), channel_id=1, source_target_pairs={{0,2},{2,0},{4,6},{6,4},{8,10},{10,8},{12,14},{14,12},{1,3},{3,1},... | collective-permute-start | bytes 30728 | tf_op jit(solution)/shard_map/ppermute | solution.py:208
  4.6 0.0 copy-done.3
  4.6 0.0 collective-permute-start.5
  4.7 1.6 %collective-permute-done.1.refs_1_ = f32[4,640]{1,0:T(4,128)S(1)} collective-permute-done((f32[4,640]{1,0:T(4,128)S(1)}, f32[4,640]{1,0:T(4,128)S(1)}, u32[]{:S(2)}, u32[]{:S(2)}) %collective-permute-start.1) | collective-permute-done | bytes 10272 | tf_op jit(solution)/shard_map/ppermute | solution.py:208
  6.3 3.2 %collective-permute-start.2 = (f32[4,640]{1,0:T(4,128)S(1)}, f32[4,640]{1,0:T(4,128)S(1)}, u32[]{:S(2)}, u32[]{:S(2)}) collective-permute-start(f32[4,640]{1,0:T(4,128)S(1)} %shard_map.111.refs_0_), channel_id=1, source_target_pairs={{0,8},{2,10},{4,12},{6,14},{8,0},{10,2},{12,4},{14,6},{1,9},{3,11}... | collective-permute-start | bytes 30728 | tf_op jit(solution)/shard_map/ppermute | solution.py:208
  9.5 0.0 copy-done.9
  9.5 0.0 copy-start.5
  9.5 0.1 collective-permute-start.7
  9.6 1.9 %collective-permute-start.8 = (bf16[64,640]{1,0:T(8,128)(2,1)S(1)}, bf16[64,640]{1,0:T(8,128)(2,1)S(1)}, u32[]{:S(2)}, u32[]{:S(2)}) collective-permute-start(bf16[64,640]{1,0:T(8,128)(2,1)S(1)} %bitcast.4), channel_id=1, source_target_pairs={{0,4},{2,6},{4,0},{6,2},{8,12},{10,14},{12,8},{14,10},{1,5},{3,7},... | collective-permute-start | bytes 245768 | tf_op jit(solution)/shard_map/ppermute | solution.py:208
  11.5 2.5 %collective-permute-start.10 = (bf16[64,640]{1,0:T(8,128)(2,1)S(1)}, bf16[64,640]{1,0:T(8,128)(2,1)S(1)}, u32[]{:S(2)}, u32[]{:S(2)}) collective-permute-start(bf16[64,640]{1,0:T(8,128)(2,1)S(1)} %bitcast.5), channel_id=1, source_target_pairs={{0,12},{2,14},{4,8},{6,10},{8,4},{10,6},{12,0},{14,2},{1,13},{3,15... | collective-permute-start | bytes 245768 | tf_op jit(solution)/shard_map/ppermute | solution.py:208
  14.0 0.0 collective-permute-done.2.refs_1_
  14.0 0.7 %collective-permute-start.3 = (f32[4,640]{1,0:T(4,128)S(1)}, f32[4,640]{1,0:T(4,128)S(1)}, u32[]{:S(2)}, u32[]{:S(2)}) collective-permute-start(f32[4,640]{1,0:T(4,128)S(1)} %shard_map.112.stat_ref), channel_id=1, source_target_pairs={{0,4},{2,6},{4,0},{6,2},{8,12},{10,14},{12,8},{14,10},{1,5},{3,7},... | collective-permute-start | bytes 30728 | tf_op jit(solution)/shard_map/ppermute | solution.py:208
  14.7 2.5 %collective-permute-done.7.refs_0_ = bf16[64,640]{1,0:T(8,128)(2,1)S(1)} collective-permute-done((bf16[64,640]{1,0:T(8,128)(2,1)S(1)}, bf16[64,640]{1,0:T(8,128)(2,1)S(1)}, u32[]{:S(2)}, u32[]{:S(2)}) %collective-permute-start.7) | collective-permute-done | bytes 81952 | tf_op jit(solution)/shard_map/ppermute | solution.py:208
  17.2 0.0 collective-permute-start.4
  17.2 0.2 shard_map.113
  17.4 0.0 collective-permute-done.8.refs_1_
  17.4 1.6 %collective-permute-start.6 = (bf16[64,640]{1,0:T(8,128)(2,1)S(1)}, bf16[64,640]{1,0:T(8,128)(2,1)S(1)}, u32[]{:S(2)}, u32[]{:S(2)}) collective-permute-start(bf16[64,640]{1,0:T(8,128)(2,1)S(1)} %bitcast.6), channel_id=1, source_target_pairs={{0,2},{2,0},{4,6},{6,4},{8,10},{10,8},{12,14},{14,12},{1,3},{3,1},... | collective-permute-start | bytes 245768 | tf_op jit(solution)/shard_map/ppermute | solution.py:208
  19.0 0.0 collective-permute-done.4.refs_4_
  19.0 0.9 %collective-permute-start.9 = (bf16[128,640]{1,0:T(8,128)(2,1)S(1)}, bf16[128,640]{1,0:T(8,128)(2,1)S(1)}, u32[]{:S(2)}, u32[]{:S(2)}) collective-permute-start(bf16[128,640]{1,0:T(8,128)(2,1)S(1)} %shard_map.115.refs_1_), channel_id=1, source_target_pairs={{0,2},{2,0},{4,6},{6,4},{8,10},{10,8},{12,14},{14,12},{1,3},{3,1},... | collective-permute-start | bytes 491528 | tf_op jit(solution)/shard_map/ppermute | solution.py:208
  19.9 0.0 collective-permute-done.10.refs_3_
  19.9 1.2 %collective-permute-start.11 = (bf16[64,640]{1,0:T(8,128)(2,1)S(1)}, bf16[64,640]{1,0:T(8,128)(2,1)S(1)}, u32[]{:S(2)}, u32[]{:S(2)}) collective-permute-start(bf16[64,640]{1,0:T(8,128)(2,1)S(1)} %collective-permute-done.10.refs_3_), channel_id=1, source_target_pairs={{0,2},{2,0},{4,6},{6,4},{8,10},{10,8},{12,14},{14,12},{1,3},{3,1},... | collective-permute-start | bytes 245768 | tf_op jit(solution)/shard_map/ppermute | solution.py:208
  21.1 0.0 collective-permute-done.3.refs_0_
  21.1 0.0 collective-permute-done.5.refs_6_
  21.1 0.0 slice-done
  21.1 0.0 slice-done.1
  21.1 0.0 copy-done.4
  21.2 0.0 copy-done.5
  21.2 0.0 copy-start
  21.2 1.7 %shard_map.114 = (bf16[32,640]{1,0:T(8,128)(2,1)S(1)}, bf16[3,32,640]{2,1,0:T(8,128)(2,1)S(1)}) custom-call(f32[4,640]{1,0:T(4,128)S(1)} %collective-permute-done.3.refs_0_, f32[4,640]{1,0:T(4,128)S(1)} %get-tuple-element.14.refs_1_, f32[32,1280]{1,0:T(8,128)S(1)} %get-tuple-element.15.refs_2_, f32[3,640]{1,0:T(4,128)S(1)} %get-tuple-element.16.refs_3_, ...), custom_call_target="tpu_custom_call" | custom-call | flops 10000000000 | bytes 131072 | tf_op jit(solution)/shard_map/pallas_call | solution.py:241
  22.9 0.0 copy-start.2
  22.9 0.0 collective-permute-done.6.refs_0_
  23.0 4.7 %collective-permute-done.11.refs_4_ = bf16[64,640]{1,0:T(8,128)(2,1)S(1)} collective-permute-done((bf16[64,640]{1,0:T(8,128)(2,1)S(1)}, bf16[64,640]{1,0:T(8,128)(2,1)S(1)}, u32[]{:S(2)}, u32[]{:S(2)}) %collective-permute-start.11) | collective-permute-done | bytes 81952 | tf_op jit(solution)/shard_map/ppermute | solution.py:208
  27.6 0.0 collective-permute-done.9.refs_2_
  27.6 0.0 copy-done
  27.6 0.6 %shard_map.116 = (bf16[32,640]{1,0:T(8,128)(2,1)S(1)}, f32[32,640]{1,0:T(8,128)S(1)}) custom-call(bf16[3,32,640]{2,1,0:T(8,128)(2,1)S(1)} %get-tuple-element.17.qkv_ref, bf16[64,640]{1,0:T(8,128)(2,1)S(1)} %collective-permute-done.6.refs_0_, bf16[128,640]{1,0:T(8,128)(2,1)S(1)} %shard_map.115.refs_1_, bf16[128,640]{1,0:T(8,128)(2,1)S(1)} %collective-permute-done.9.refs_2_, ...), custom_call_target="tpu_custom_call" | custom-call | bytes 131072 | tf_op jit(solution)/shard_map/pallas_call | solution.py:253
  28.3 0.1 collective-permute-start.12
  28.3 0.0 copy-done.2
  28.4 0.3 shard_map.117
  28.6 1.0 %collective-permute-done.12 = f32[32,640]{1,0:T(8,128)S(1)} collective-permute-done((f32[32,640]{1,0:T(8,128)S(1)}, f32[32,640]{1,0:T(8,128)S(1)}, u32[]{:S(2)}, u32[]{:S(2)}) %collective-permute-start.12) | collective-permute-done | bytes 81952 | tf_op jit(solution)/shard_map/ppermute | solution.py:208
  29.6 0.6 %add.3 = f32[32,640]{1,0:T(8,128)} add(f32[32,640]{1,0:T(8,128)S(1)} %shard_map.117, f32[32,640]{1,0:T(8,128)S(1)} %collective-permute-done.12) | non-fusion elementwise | flops 20480 | bytes 245760 | tf_op jit(solution)/shard_map/add | solution.py:261
  (13 shorter events, 0.1 us)
Async XLA Ops:
  0.0 1.7 %copy-start.1 = (bf16[32,640]{1,0:T(8,128)(2,1)S(1)}, bf16[32,640]{1,0:T(8,128)(2,1)}, u32[]{:S(2)}) copy-start(bf16[32,640]{1,0:T(8,128)(2,1)} %own_ref.3) | copy-start | bytes 122884
  0.0 1.7 %copy-start.6 = (f32[640]{0:T(1024)S(1)}, f32[640]{0:T(1024)}, u32[]{:S(2)}) copy-start(f32[640]{0:T(1024)} %gain_ref.1) | copy-start | bytes 7684
  0.0 1.7 %copy-start.7 = (f32[640]{0:T(1024)S(1)}, f32[640]{0:T(1024)}, u32[]{:S(2)}) copy-start(f32[640]{0:T(1024)} %bias_ref.1) | copy-start | bytes 7684
  0.0 1.7 %copy-start.8 = (f32[640]{0:T(1024)S(1)}, f32[640]{0:T(1024)}, u32[]{:S(2)}) copy-start(f32[640]{0:T(1024)} %b_in_ref.1) | copy-start | bytes 7684
  0.0 1.6 %collective-permute-start = (bf16[32,640]{1,0:T(8,128)(2,1)}, bf16[32,640]{1,0:T(8,128)(2,1)S(1)}, u32[]{:S(2)}, u32[]{:S(2)}) collective-permute-start(bf16[32,640]{1,0:T(8,128)(2,1)} %own_ref.3), channel_id=1, source_target_pairs={{0,1},{1,0},{2,3},{3,2},{4,5},{5,4},{6,7},{7,6},{8,9},{9,8},{10,11... | collective-permute-start | bytes 122888 | tf_op jit(solution)/shard_map/ppermute | solution.py:208
  0.6 4.1 %copy-start.3 = (bf16[1280,640]{1,0:T(8,128)(2,1)S(1)}, bf16[1280,640]{1,0:T(8,128)(2,1)}, u32[]{:S(2)}) copy-start(bf16[1280,640]{1,0:T(8,128)(2,1)} %refs_5_.2) | copy-start | bytes 4915204
  1.7 7.8 %copy-start.9 = (bf16[2,32,640]{2,1,0:T(8,128)(2,1)S(1)}, bf16[2,32,640]{2,1,0:T(8,128)(2,1)}, u32[]{:S(2)}) copy-start(bf16[2,32,640]{2,1,0:T(8,128)(2,1)} %param.19) | copy-start | bytes 245764
  1.8 4.5 %collective-permute-start.1 = (f32[4,640]{1,0:T(4,128)S(1)}, f32[4,640]{1,0:T(4,128)S(1)}, u32[]{:S(2)}, u32[]{:S(2)}) collective-permute-start(f32[4,640]{1,0:T(4,128)S(1)} %get-tuple-element.13.refs_0_), channel_id=1, source_target_pairs={{0,2},{2,0},{4,6},{6,4},{8,10},{10,8},{12,14},{14,12},{1,3},{3,1},... | collective-permute-start | bytes 30728 | tf_op jit(solution)/shard_map/ppermute | solution.py:208
  4.6 16.5 %collective-permute-start.5 = (bf16[1280,640]{1,0:T(8,128)(2,1)S(1)}, bf16[1280,640]{1,0:T(8,128)(2,1)S(1)}, u32[]{:S(2)}, u32[]{:S(2)}) collective-permute-start(bf16[1280,640]{1,0:T(8,128)(2,1)S(1)} %copy-done.3), channel_id=1, source_target_pairs={{0,1},{1,0},{2,3},{3,2},{4,5},{5,4},{6,7},{7,6},{8,9},{9,8},{10,11... | collective-permute-start | bytes 4915208 | tf_op jit(solution)/shard_map/ppermute | solution.py:208
  6.3 7.7 %collective-permute-start.2 = (f32[4,640]{1,0:T(4,128)S(1)}, f32[4,640]{1,0:T(4,128)S(1)}, u32[]{:S(2)}, u32[]{:S(2)}) collective-permute-start(f32[4,640]{1,0:T(4,128)S(1)} %shard_map.111.refs_0_), channel_id=1, source_target_pairs={{0,8},{2,10},{4,12},{6,14},{8,0},{10,2},{12,4},{14,6},{1,9},{3,11}... | collective-permute-start | bytes 30728 | tf_op jit(solution)/shard_map/ppermute | solution.py:208
  9.5 11.6 %slice-start = ((s8[4915200]{0:T(1024)(128)(4,1)}), s8[4194304]{0:T(1024)(128)(4,1)S(1)}, s32[]{:S(2)}) async-start(s8[4915200]{0:T(1024)(128)(4,1)} %bitcast.1), calls=%async_computation | async-start | bytes 8388608
  9.5 11.6 %slice-start.1 = ((s8[4915200]{0:T(1024)(128)(4,1)}), s8[720896]{0:T(1024)(128)(4,1)S(1)}, s32[]{:S(2)}) async-start(s8[4915200]{0:T(1024)(128)(4,1)} %bitcast.1), calls=%async_computation.1 | async-start | bytes 1441792
  9.5 11.6 %copy-start.4 = (f32[1280]{0:T(1024)S(1)}, f32[1280]{0:T(1024)}, u32[]{:S(2)}) copy-start(f32[1280]{0:T(1024)} %refs_7_.1) | copy-start | bytes 15364
  9.5 11.6 %copy-start.5 = (f32[1280]{0:T(1024)S(1)}, f32[1280]{0:T(1024)}, u32[]{:S(2)}) copy-start(f32[1280]{0:T(1024)} %refs_8_.1) | copy-start | bytes 15364
  9.5 7.7 %collective-permute-start.7 = (bf16[64,640]{1,0:T(8,128)(2,1)S(1)}, bf16[64,640]{1,0:T(8,128)(2,1)S(1)}, u32[]{:S(2)}, u32[]{:S(2)}) collective-permute-start(bf16[64,640]{1,0:T(8,128)(2,1)S(1)} %bitcast.3), channel_id=1, source_target_pairs={{0,8},{2,10},{4,12},{6,14},{8,0},{10,2},{12,4},{14,6},{1,9},{3,11}... | collective-permute-start | bytes 245768 | tf_op jit(solution)/shard_map/ppermute | solution.py:208
  9.6 7.8 %collective-permute-start.8 = (bf16[64,640]{1,0:T(8,128)(2,1)S(1)}, bf16[64,640]{1,0:T(8,128)(2,1)S(1)}, u32[]{:S(2)}, u32[]{:S(2)}) collective-permute-start(bf16[64,640]{1,0:T(8,128)(2,1)S(1)} %bitcast.4), channel_id=1, source_target_pairs={{0,4},{2,6},{4,0},{6,2},{8,12},{10,14},{12,8},{14,10},{1,5},{3,7},... | collective-permute-start | bytes 245768 | tf_op jit(solution)/shard_map/ppermute | solution.py:208
  11.5 8.4 %collective-permute-start.10 = (bf16[64,640]{1,0:T(8,128)(2,1)S(1)}, bf16[64,640]{1,0:T(8,128)(2,1)S(1)}, u32[]{:S(2)}, u32[]{:S(2)}) collective-permute-start(bf16[64,640]{1,0:T(8,128)(2,1)S(1)} %bitcast.5), channel_id=1, source_target_pairs={{0,12},{2,14},{4,8},{6,10},{8,4},{10,6},{12,0},{14,2},{1,13},{3,15... | collective-permute-start | bytes 245768 | tf_op jit(solution)/shard_map/ppermute | solution.py:208
  14.0 7.1 %collective-permute-start.3 = (f32[4,640]{1,0:T(4,128)S(1)}, f32[4,640]{1,0:T(4,128)S(1)}, u32[]{:S(2)}, u32[]{:S(2)}) collective-permute-start(f32[4,640]{1,0:T(4,128)S(1)} %shard_map.112.stat_ref), channel_id=1, source_target_pairs={{0,4},{2,6},{4,0},{6,2},{8,12},{10,14},{12,8},{14,10},{1,5},{3,7},... | collective-permute-start | bytes 30728 | tf_op jit(solution)/shard_map/ppermute | solution.py:208
  17.2 1.8 %collective-permute-start.4 = (f32[3,640]{1,0:T(4,128)S(1)}, f32[3,640]{1,0:T(4,128)S(1)}, u32[]{:S(2)}, u32[]{:S(2)}) collective-permute-start(f32[3,640]{1,0:T(4,128)S(1)} %get-tuple-element.16.refs_3_), channel_id=1, source_target_pairs={{0,1},{1,0},{2,3},{3,2},{4,5},{5,4},{6,7},{7,6},{8,9},{9,8},{10,11... | collective-permute-start | bytes 23048 | tf_op jit(solution)/shard_map/ppermute | solution.py:208
  17.4 5.5 %collective-permute-start.6 = (bf16[64,640]{1,0:T(8,128)(2,1)S(1)}, bf16[64,640]{1,0:T(8,128)(2,1)S(1)}, u32[]{:S(2)}, u32[]{:S(2)}) collective-permute-start(bf16[64,640]{1,0:T(8,128)(2,1)S(1)} %bitcast.6), channel_id=1, source_target_pairs={{0,2},{2,0},{4,6},{6,4},{8,10},{10,8},{12,14},{14,12},{1,3},{3,1},... | collective-permute-start | bytes 245768 | tf_op jit(solution)/shard_map/ppermute | solution.py:208
  19.0 8.6 %collective-permute-start.9 = (bf16[128,640]{1,0:T(8,128)(2,1)S(1)}, bf16[128,640]{1,0:T(8,128)(2,1)S(1)}, u32[]{:S(2)}, u32[]{:S(2)}) collective-permute-start(bf16[128,640]{1,0:T(8,128)(2,1)S(1)} %shard_map.115.refs_1_), channel_id=1, source_target_pairs={{0,2},{2,0},{4,6},{6,4},{8,10},{10,8},{12,14},{14,12},{1,3},{3,1},... | collective-permute-start | bytes 491528 | tf_op jit(solution)/shard_map/ppermute | solution.py:208
  19.9 7.7 %collective-permute-start.11 = (bf16[64,640]{1,0:T(8,128)(2,1)S(1)}, bf16[64,640]{1,0:T(8,128)(2,1)S(1)}, u32[]{:S(2)}, u32[]{:S(2)}) collective-permute-start(bf16[64,640]{1,0:T(8,128)(2,1)S(1)} %collective-permute-done.10.refs_3_), channel_id=1, source_target_pairs={{0,2},{2,0},{4,6},{6,4},{8,10},{10,8},{12,14},{14,12},{1,3},{3,1},... | collective-permute-start | bytes 245768 | tf_op jit(solution)/shard_map/ppermute | solution.py:208
  21.2 6.5 %copy-start = (bf16[640,1280]{1,0:T(8,128)(2,1)S(1)}, bf16[640,1280]{1,0:T(8,128)(2,1)}, u32[]{:S(2)}) copy-start(bf16[640,1280]{1,0:T(8,128)(2,1)} %w_ref.1) | copy-start | bytes 4915204
  22.9 5.4 %copy-start.2 = (f32[640]{0:T(1024)S(1)}, f32[640]{0:T(1024)}, u32[]{:S(2)}) copy-start(f32[640]{0:T(1024)} %b_ref.1) | copy-start | bytes 7684
  28.3 1.3 %collective-permute-start.12 = (f32[32,640]{1,0:T(8,128)S(1)}, f32[32,640]{1,0:T(8,128)S(1)}, u32[]{:S(2)}, u32[]{:S(2)}) collective-permute-start(f32[32,640]{1,0:T(8,128)S(1)} %get-tuple-element.20), channel_id=1, source_target_pairs={{0,1},{1,0},{2,3},{3,2},{4,5},{5,4},{6,7},{7,6},{8,9},{9,8},{10,11... | collective-permute-start | bytes 245768 | tf_op jit(solution)/shard_map/ppermute | solution.py:208

commit v2 on v1

--- a/solution.py
+++ b/solution.py
@@ -184,7 +184,7 @@
     att = jnp.concatenate(att, axis=1)
     att_ref[...] = att
     first = pl.multiple_of((1 - lax.axis_index("heads")) * width, 128)
-    send_ref[...] = jnp.dot(att, w_ref[:, pl.ds(first, width)], preferred_element_type=F32)
+    send_ref[...] = jnp.dot(att, w_ref[:, pl.ds(first, width)], preferred_element_type=F32).astype(BF)
 
 
 def own_kernel(att_ref, stream_ref, b_ref, w_ref, out_ref):
@@ -252,13 +252,13 @@
         sources = [(0, 0, n_keys, n_keys, False)]
     attended, send = call(
         functools.partial(attn_kernel, sources),
-        (sds((tok, width), BF), sds((tok, width), F32)),
+        (sds((tok, width), BF), sds((tok, width), BF)),
         2 + len(strips),
         extra=64 * tok * n_keys + 4 * n_keys * width,
     )(qkv, *strips, w_out)
     received = move(send, 0)
     mine = call(own_kernel, sds((tok, width), F32), 4)(attended, stream, b_out, w_out)
-    return mine + received
+    return mine + received.astype(F32)
 
 
 def solution(mesh):

time: 30.4 us -> 30.3 us (level)
  transfers between devices with their start and end apart: 13 -> 13, of which waited for: 5 -> 5; matrix products, arithmetic and copies ran while one was open for 0% -> 0% of each run, Pallas kernels for 7% -> 8%
where the time goes in v2:
time: 30.3 us; the launch traced here: 30.2 us
  starting transfers between devices  15.6 us (51%)
  waiting for transfers between devices  10.8 us (36%)
  Pallas kernels  2.96 us (10%)
  other arithmetic  0.65 us (2%)
    ppermute x9, starting transfers between devices, move(): lax.ppermute(x, 'patch', partner(k))  14.9 us
    ppermute x9, waiting for transfers between devices, move(): lax.ppermute(x, 'patch', partner(k))  8.8 us
    ppermute x4, waiting for transfers between devices, move(): lax.ppermute(x, 'heads', swap)  2.01 us
    pallas_call x1, Pallas kernels, body(): call(functools.partial(front_kernel, count, group_size, len(stats) - 1),...  1.75 us
    add x1, other arithmetic, body(): return mine + received.astype(F32)  0.65 us
    ppermute x4, starting transfers between devices, move(): lax.ppermute(x, 'heads', swap)  0.64 us
    pallas_call x1, Pallas kernels, body(): call(functools.partial(attn_kernel, sources), (sds((tok, width), BF), sds...  0.63 us
  transfers between devices with their start and end apart: 13, of which 5 were waited for; matrix products, arithmetic and copies ran while one was open for 0% of the time, Pallas kernels for 8%

profile of v2, /device:TPU:0, one launch (start us, length us, event | category | flops | bytes accessed | tf_op | source)
XLA Modules:
  0.0 30.2 jit_solution(5198364464922799216)
XLA Ops:
  0.0 0.6 %collective-permute-start = (bf16[32,640]{1,0:T(8,128)(2,1)}, bf16[32,640]{1,0:T(8,128)(2,1)S(1)}, u32[]{:S(2)}, u32[]{:S(2)}) collective-permute-start(bf16[32,640]{1,0:T(8,128)(2,1)} %own_ref.3), channel_id=1, source_target_pairs={{0,1},{1,0},{2,3},{3,2},{4,5},{5,4},{6,7},{7,6},{8,9},{9,8},{10,11... | collective-permute-start | bytes 122888 | tf_op jit(solution)/shard_map/ppermute | solution.py:208
  0.6 1.1 %collective-permute-done.other_ref = bf16[32,640]{1,0:T(8,128)(2,1)S(1)} collective-permute-done((bf16[32,640]{1,0:T(8,128)(2,1)}, bf16[32,640]{1,0:T(8,128)(2,1)S(1)}, u32[]{:S(2)}, u32[]{:S(2)}) %collective-permute-start) | collective-permute-done | bytes 40992 | tf_op jit(solution)/shard_map/ppermute | solution.py:208
  1.7 0.0 copy-done.1
  1.7 0.0 copy-done.6
  1.7 0.0 copy-done.7
  1.7 0.0 copy-done.8
  1.7 0.1 shard_map.110
  1.7 0.0 copy-start.9
  1.8 2.9 %collective-permute-start.1 = (f32[4,640]{1,0:T(4,128)S(1)}, f32[4,640]{1,0:T(4,128)S(1)}, u32[]{:S(2)}, u32[]{:S(2)}) collective-permute-start(f32[4,640]{1,0:T(4,128)S(1)} %get-tuple-element.13.refs_0_), channel_id=1, source_target_pairs={{0,2},{2,0},{4,6},{6,4},{8,10},{10,8},{12,14},{14,12},{1,3},{3,1},... | collective-permute-start | bytes 30728 | tf_op jit(solution)/shard_map/ppermute | solution.py:208
  4.6 0.0 copy-done.3
  4.6 0.0 collective-permute-start.5
  4.7 1.6 %collective-permute-done.1.refs_1_ = f32[4,640]{1,0:T(4,128)S(1)} collective-permute-done((f32[4,640]{1,0:T(4,128)S(1)}, f32[4,640]{1,0:T(4,128)S(1)}, u32[]{:S(2)}, u32[]{:S(2)}) %collective-permute-start.1) | collective-permute-done | bytes 10272 | tf_op jit(solution)/shard_map/ppermute | solution.py:208
  6.3 3.2 %collective-permute-start.2 = (f32[4,640]{1,0:T(4,128)S(1)}, f32[4,640]{1,0:T(4,128)S(1)}, u32[]{:S(2)}, u32[]{:S(2)}) collective-permute-start(f32[4,640]{1,0:T(4,128)S(1)} %shard_map.111.refs_0_), channel_id=1, source_target_pairs={{0,8},{2,10},{4,12},{6,14},{8,0},{10,2},{12,4},{14,6},{1,9},{3,11}... | collective-permute-start | bytes 30728 | tf_op jit(solution)/shard_map/ppermute | solution.py:208
  9.5 0.0 copy-done.9
  9.5 0.0 copy-start.5
  9.5 0.1 collective-permute-start.7
  9.6 1.9 %collective-permute-start.8 = (bf16[64,640]{1,0:T(8,128)(2,1)S(1)}, bf16[64,640]{1,0:T(8,128)(2,1)S(1)}, u32[]{:S(2)}, u32[]{:S(2)}) collective-permute-start(bf16[64,640]{1,0:T(8,128)(2,1)S(1)} %bitcast.4), channel_id=1, source_target_pairs={{0,4},{2,6},{4,0},{6,2},{8,12},{10,14},{12,8},{14,10},{1,5},{3,7},... | collective-permute-start | bytes 245768 | tf_op jit(solution)/shard_map/ppermute | solution.py:208
  11.5 2.5 %collective-permute-start.10 = (bf16[64,640]{1,0:T(8,128)(2,1)S(1)}, bf16[64,640]{1,0:T(8,128)(2,1)S(1)}, u32[]{:S(2)}, u32[]{:S(2)}) collective-permute-start(bf16[64,640]{1,0:T(8,128)(2,1)S(1)} %bitcast.5), channel_id=1, source_target_pairs={{0,12},{2,14},{4,8},{6,10},{8,4},{10,6},{12,0},{14,2},{1,13},{3,15... | collective-permute-start | bytes 245768 | tf_op jit(solution)/shard_map/ppermute | solution.py:208
  14.0 0.0 collective-permute-done.2.refs_1_
  14.0 0.7 %collective-permute-start.3 = (f32[4,640]{1,0:T(4,128)S(1)}, f32[4,640]{1,0:T(4,128)S(1)}, u32[]{:S(2)}, u32[]{:S(2)}) collective-permute-start(f32[4,640]{1,0:T(4,128)S(1)} %shard_map.112.stat_ref), channel_id=1, source_target_pairs={{0,4},{2,6},{4,0},{6,2},{8,12},{10,14},{12,8},{14,10},{1,5},{3,7},... | collective-permute-start | bytes 30728 | tf_op jit(solution)/shard_map/ppermute | solution.py:208
  14.7 2.5 %collective-permute-done.7.refs_0_ = bf16[64,640]{1,0:T(8,128)(2,1)S(1)} collective-permute-done((bf16[64,640]{1,0:T(8,128)(2,1)S(1)}, bf16[64,640]{1,0:T(8,128)(2,1)S(1)}, u32[]{:S(2)}, u32[]{:S(2)}) %collective-permute-start.7) | collective-permute-done | bytes 81952 | tf_op jit(solution)/shard_map/ppermute | solution.py:208
  17.2 0.0 collective-permute-start.4
  17.2 0.2 shard_map.113
  17.4 0.0 collective-permute-done.8.refs_1_
  17.4 1.6 %collective-permute-start.6 = (bf16[64,640]{1,0:T(8,128)(2,1)S(1)}, bf16[64,640]{1,0:T(8,128)(2,1)S(1)}, u32[]{:S(2)}, u32[]{:S(2)}) collective-permute-start(bf16[64,640]{1,0:T(8,128)(2,1)S(1)} %bitcast.6), channel_id=1, source_target_pairs={{0,2},{2,0},{4,6},{6,4},{8,10},{10,8},{12,14},{14,12},{1,3},{3,1},... | collective-permute-start | bytes 245768 | tf_op jit(solution)/shard_map/ppermute | solution.py:208
  19.0 0.0 collective-permute-done.4.refs_4_
  19.0 0.9 %collective-permute-start.9 = (bf16[128,640]{1,0:T(8,128)(2,1)S(1)}, bf16[128,640]{1,0:T(8,128)(2,1)S(1)}, u32[]{:S(2)}, u32[]{:S(2)}) collective-permute-start(bf16[128,640]{1,0:T(8,128)(2,1)S(1)} %shard_map.115.refs_1_), channel_id=1, source_target_pairs={{0,2},{2,0},{4,6},{6,4},{8,10},{10,8},{12,14},{14,12},{1,3},{3,1},... | collective-permute-start | bytes 491528 | tf_op jit(solution)/shard_map/ppermute | solution.py:208
  19.9 0.0 collective-permute-done.10.refs_3_
  19.9 1.2 %collective-permute-start.11 = (bf16[64,640]{1,0:T(8,128)(2,1)S(1)}, bf16[64,640]{1,0:T(8,128)(2,1)S(1)}, u32[]{:S(2)}, u32[]{:S(2)}) collective-permute-start(bf16[64,640]{1,0:T(8,128)(2,1)S(1)} %collective-permute-done.10.refs_3_), channel_id=1, source_target_pairs={{0,2},{2,0},{4,6},{6,4},{8,10},{10,8},{12,14},{14,12},{1,3},{3,1},... | collective-permute-start | bytes 245768 | tf_op jit(solution)/shard_map/ppermute | solution.py:208
  21.1 0.0 collective-permute-done.3.refs_0_
  21.1 0.0 collective-permute-done.5.refs_6_
  21.1 0.0 slice-done
  21.1 0.0 slice-done.1
  21.1 0.0 copy-done.4
  21.2 0.0 copy-done.5
  21.2 0.0 copy-start
  21.2 1.7 %shard_map.114 = (bf16[32,640]{1,0:T(8,128)(2,1)S(1)}, bf16[3,32,640]{2,1,0:T(8,128)(2,1)S(1)}) custom-call(f32[4,640]{1,0:T(4,128)S(1)} %collective-permute-done.3.refs_0_, f32[4,640]{1,0:T(4,128)S(1)} %get-tuple-element.14.refs_1_, f32[32,1280]{1,0:T(8,128)S(1)} %get-tuple-element.15.refs_2_, f32[3,640]{1,0:T(4,128)S(1)} %get-tuple-element.16.refs_3_, ...), custom_call_target="tpu_custom_call" | custom-call | flops 10000000000 | bytes 131072 | tf_op jit(solution)/shard_map/pallas_call | solution.py:241
  22.9 0.0 copy-start.2
  22.9 0.0 collective-permute-done.6.refs_0_
  23.0 4.7 %collective-permute-done.11.refs_4_ = bf16[64,640]{1,0:T(8,128)(2,1)S(1)} collective-permute-done((bf16[64,640]{1,0:T(8,128)(2,1)S(1)}, bf16[64,640]{1,0:T(8,128)(2,1)S(1)}, u32[]{:S(2)}, u32[]{:S(2)}) %collective-permute-start.11) | collective-permute-done | bytes 81952 | tf_op jit(solution)/shard_map/ppermute | solution.py:208
  27.6 0.0 collective-permute-done.9.refs_2_
  27.6 0.0 copy-done
  27.6 0.6 %shard_map.116 = (bf16[32,640]{1,0:T(8,128)(2,1)S(1)}, bf16[32,640]{1,0:T(8,128)(2,1)S(1)}) custom-call(bf16[3,32,640]{2,1,0:T(8,128)(2,1)S(1)} %get-tuple-element.17.qkv_ref, bf16[64,640]{1,0:T(8,128)(2,1)S(1)} %collective-permute-done.6.refs_0_, bf16[128,640]{1,0:T(8,128)(2,1)S(1)} %shard_map.115.refs_1_, ...), custom_call_target="tpu_custom_call" | custom-call | bytes 131072 | tf_op jit(solution)/shard_map/pallas_call | solution.py:253
  28.3 0.1 collective-permute-start.12
  28.4 0.0 copy-done.2
  28.4 0.3 shard_map.117
  28.6 0.9 %collective-permute-done.12 = bf16[32,640]{1,0:T(8,128)(2,1)S(1)} collective-permute-done((bf16[32,640]{1,0:T(8,128)(2,1)S(1)}, bf16[32,640]{1,0:T(8,128)(2,1)S(1)}, u32[]{:S(2)}, u32[]{:S(2)}) %collective-permute-start.12) | collective-permute-done | bytes 40992 | tf_op jit(solution)/shard_map/ppermute | solution.py:208
  29.6 0.6 %convert_add_fusion = f32[32,640]{1,0:T(8,128)} fusion(f32[32,640]{1,0:T(8,128)S(1)} %shard_map.117, bf16[32,640]{1,0:T(8,128)(2,1)S(1)} %collective-permute-done.12), kind=kLoop, calls=%fused_computation | loop fusion | flops 40960 | bytes 204800 | tf_op jit(solution)/shard_map/add | solution.py:261
  (13 shorter events, 0.1 us)
Async XLA Ops:
  0.0 1.7 %copy-start.1 = (bf16[32,640]{1,0:T(8,128)(2,1)S(1)}, bf16[32,640]{1,0:T(8,128)(2,1)}, u32[]{:S(2)}) copy-start(bf16[32,640]{1,0:T(8,128)(2,1)} %own_ref.3) | copy-start | bytes 122884
  0.0 1.7 %copy-start.6 = (f32[640]{0:T(1024)S(1)}, f32[640]{0:T(1024)}, u32[]{:S(2)}) copy-start(f32[640]{0:T(1024)} %gain_ref.1) | copy-start | bytes 7684
  0.0 1.7 %copy-start.7 = (f32[640]{0:T(1024)S(1)}, f32[640]{0:T(1024)}, u32[]{:S(2)}) copy-start(f32[640]{0:T(1024)} %bias_ref.1) | copy-start | bytes 7684
  0.0 1.7 %copy-start.8 = (f32[640]{0:T(1024)S(1)}, f32[640]{0:T(1024)}, u32[]{:S(2)}) copy-start(f32[640]{0:T(1024)} %b_in_ref.1) | copy-start | bytes 7684
  0.0 1.6 %collective-permute-start = (bf16[32,640]{1,0:T(8,128)(2,1)}, bf16[32,640]{1,0:T(8,128)(2,1)S(1)}, u32[]{:S(2)}, u32[]{:S(2)}) collective-permute-start(bf16[32,640]{1,0:T(8,128)(2,1)} %own_ref.3), channel_id=1, source_target_pairs={{0,1},{1,0},{2,3},{3,2},{4,5},{5,4},{6,7},{7,6},{8,9},{9,8},{10,11... | collective-permute-start | bytes 122888 | tf_op jit(solution)/shard_map/ppermute | solution.py:208
  0.6 4.1 %copy-start.3 = (bf16[1280,640]{1,0:T(8,128)(2,1)S(1)}, bf16[1280,640]{1,0:T(8,128)(2,1)}, u32[]{:S(2)}) copy-start(bf16[1280,640]{1,0:T(8,128)(2,1)} %refs_5_.2) | copy-start | bytes 4915204
  1.7 7.8 %copy-start.9 = (bf16[2,32,640]{2,1,0:T(8,128)(2,1)S(1)}, bf16[2,32,640]{2,1,0:T(8,128)(2,1)}, u32[]{:S(2)}) copy-start(bf16[2,32,640]{2,1,0:T(8,128)(2,1)} %param.19) | copy-start | bytes 245764
  1.8 4.5 %collective-permute-start.1 = (f32[4,640]{1,0:T(4,128)S(1)}, f32[4,640]{1,0:T(4,128)S(1)}, u32[]{:S(2)}, u32[]{:S(2)}) collective-permute-start(f32[4,640]{1,0:T(4,128)S(1)} %get-tuple-element.13.refs_0_), channel_id=1, source_target_pairs={{0,2},{2,0},{4,6},{6,4},{8,10},{10,8},{12,14},{14,12},{1,3},{3,1},... | collective-permute-start | bytes 30728 | tf_op jit(solution)/shard_map/ppermute | solution.py:208
  4.6 16.5 %collective-permute-start.5 = (bf16[1280,640]{1,0:T(8,128)(2,1)S(1)}, bf16[1280,640]{1,0:T(8,128)(2,1)S(1)}, u32[]{:S(2)}, u32[]{:S(2)}) collective-permute-start(bf16[1280,640]{1,0:T(8,128)(2,1)S(1)} %copy-done.3), channel_id=1, source_target_pairs={{0,1},{1,0},{2,3},{3,2},{4,5},{5,4},{6,7},{7,6},{8,9},{9,8},{10,11... | collective-permute-start | bytes 4915208 | tf_op jit(solution)/shard_map/ppermute | solution.py:208
  6.3 7.7 %collective-permute-start.2 = (f32[4,640]{1,0:T(4,128)S(1)}, f32[4,640]{1,0:T(4,128)S(1)}, u32[]{:S(2)}, u32[]{:S(2)}) collective-permute-start(f32[4,640]{1,0:T(4,128)S(1)} %shard_map.111.refs_0_), channel_id=1, source_target_pairs={{0,8},{2,10},{4,12},{6,14},{8,0},{10,2},{12,4},{14,6},{1,9},{3,11}... | collective-permute-start | bytes 30728 | tf_op jit(solution)/shard_map/ppermute | solution.py:208
  9.5 11.6 %slice-start = ((s8[4915200]{0:T(1024)(128)(4,1)}), s8[4194304]{0:T(1024)(128)(4,1)S(1)}, s32[]{:S(2)}) async-start(s8[4915200]{0:T(1024)(128)(4,1)} %bitcast.1), calls=%async_computation | async-start | bytes 8388608
  9.5 11.6 %slice-start.1 = ((s8[4915200]{0:T(1024)(128)(4,1)}), s8[720896]{0:T(1024)(128)(4,1)S(1)}, s32[]{:S(2)}) async-start(s8[4915200]{0:T(1024)(128)(4,1)} %bitcast.1), calls=%async_computation.1 | async-start | bytes 1441792
  9.5 11.6 %copy-start.4 = (f32[1280]{0:T(1024)S(1)}, f32[1280]{0:T(1024)}, u32[]{:S(2)}) copy-start(f32[1280]{0:T(1024)} %refs_7_.1) | copy-start | bytes 15364
  9.5 11.6 %copy-start.5 = (f32[1280]{0:T(1024)S(1)}, f32[1280]{0:T(1024)}, u32[]{:S(2)}) copy-start(f32[1280]{0:T(1024)} %refs_8_.1) | copy-start | bytes 15364
  9.5 7.7 %collective-permute-start.7 = (bf16[64,640]{1,0:T(8,128)(2,1)S(1)}, bf16[64,640]{1,0:T(8,128)(2,1)S(1)}, u32[]{:S(2)}, u32[]{:S(2)}) collective-permute-start(bf16[64,640]{1,0:T(8,128)(2,1)S(1)} %bitcast.3), channel_id=1, source_target_pairs={{0,8},{2,10},{4,12},{6,14},{8,0},{10,2},{12,4},{14,6},{1,9},{3,11}... | collective-permute-start | bytes 245768 | tf_op jit(solution)/shard_map/ppermute | solution.py:208
  9.6 7.8 %collective-permute-start.8 = (bf16[64,640]{1,0:T(8,128)(2,1)S(1)}, bf16[64,640]{1,0:T(8,128)(2,1)S(1)}, u32[]{:S(2)}, u32[]{:S(2)}) collective-permute-start(bf16[64,640]{1,0:T(8,128)(2,1)S(1)} %bitcast.4), channel_id=1, source_target_pairs={{0,4},{2,6},{4,0},{6,2},{8,12},{10,14},{12,8},{14,10},{1,5},{3,7},... | collective-permute-start | bytes 245768 | tf_op jit(solution)/shard_map/ppermute | solution.py:208
  11.5 8.4 %collective-permute-start.10 = (bf16[64,640]{1,0:T(8,128)(2,1)S(1)}, bf16[64,640]{1,0:T(8,128)(2,1)S(1)}, u32[]{:S(2)}, u32[]{:S(2)}) collective-permute-start(bf16[64,640]{1,0:T(8,128)(2,1)S(1)} %bitcast.5), channel_id=1, source_target_pairs={{0,12},{2,14},{4,8},{6,10},{8,4},{10,6},{12,0},{14,2},{1,13},{3,15... | collective-permute-start | bytes 245768 | tf_op jit(solution)/shard_map/ppermute | solution.py:208
  14.0 7.1 %collective-permute-start.3 = (f32[4,640]{1,0:T(4,128)S(1)}, f32[4,640]{1,0:T(4,128)S(1)}, u32[]{:S(2)}, u32[]{:S(2)}) collective-permute-start(f32[4,640]{1,0:T(4,128)S(1)} %shard_map.112.stat_ref), channel_id=1, source_target_pairs={{0,4},{2,6},{4,0},{6,2},{8,12},{10,14},{12,8},{14,10},{1,5},{3,7},... | collective-permute-start | bytes 30728 | tf_op jit(solution)/shard_map/ppermute | solution.py:208
  17.2 1.8 %collective-permute-start.4 = (f32[3,640]{1,0:T(4,128)S(1)}, f32[3,640]{1,0:T(4,128)S(1)}, u32[]{:S(2)}, u32[]{:S(2)}) collective-permute-start(f32[3,640]{1,0:T(4,128)S(1)} %get-tuple-element.16.refs_3_), channel_id=1, source_target_pairs={{0,1},{1,0},{2,3},{3,2},{4,5},{5,4},{6,7},{7,6},{8,9},{9,8},{10,11... | collective-permute-start | bytes 23048 | tf_op jit(solution)/shard_map/ppermute | solution.py:208
  17.4 5.5 %collective-permute-start.6 = (bf16[64,640]{1,0:T(8,128)(2,1)S(1)}, bf16[64,640]{1,0:T(8,128)(2,1)S(1)}, u32[]{:S(2)}, u32[]{:S(2)}) collective-permute-start(bf16[64,640]{1,0:T(8,128)(2,1)S(1)} %bitcast.6), channel_id=1, source_target_pairs={{0,2},{2,0},{4,6},{6,4},{8,10},{10,8},{12,14},{14,12},{1,3},{3,1},... | collective-permute-start | bytes 245768 | tf_op jit(solution)/shard_map/ppermute | solution.py:208
  19.0 8.6 %collective-permute-start.9 = (bf16[128,640]{1,0:T(8,128)(2,1)S(1)}, bf16[128,640]{1,0:T(8,128)(2,1)S(1)}, u32[]{:S(2)}, u32[]{:S(2)}) collective-permute-start(bf16[128,640]{1,0:T(8,128)(2,1)S(1)} %shard_map.115.refs_1_), channel_id=1, source_target_pairs={{0,2},{2,0},{4,6},{6,4},{8,10},{10,8},{12,14},{14,12},{1,3},{3,1},... | collective-permute-start | bytes 491528 | tf_op jit(solution)/shard_map/ppermute | solution.py:208
  19.9 7.7 %collective-permute-start.11 = (bf16[64,640]{1,0:T(8,128)(2,1)S(1)}, bf16[64,640]{1,0:T(8,128)(2,1)S(1)}, u32[]{:S(2)}, u32[]{:S(2)}) collective-permute-start(bf16[64,640]{1,0:T(8,128)(2,1)S(1)} %collective-permute-done.10.refs_3_), channel_id=1, source_target_pairs={{0,2},{2,0},{4,6},{6,4},{8,10},{10,8},{12,14},{14,12},{1,3},{3,1},... | collective-permute-start | bytes 245768 | tf_op jit(solution)/shard_map/ppermute | solution.py:208
  21.2 6.5 %copy-start = (bf16[640,1280]{1,0:T(8,128)(2,1)S(1)}, bf16[640,1280]{1,0:T(8,128)(2,1)}, u32[]{:S(2)}) copy-start(bf16[640,1280]{1,0:T(8,128)(2,1)} %w_ref.1) | copy-start | bytes 4915204
  22.9 5.4 %copy-start.2 = (f32[640]{0:T(1024)S(1)}, f32[640]{0:T(1024)}, u32[]{:S(2)}) copy-start(f32[640]{0:T(1024)} %b_ref.1) | copy-start | bytes 7684
  28.3 1.3 %collective-permute-start.12 = (bf16[32,640]{1,0:T(8,128)(2,1)S(1)}, bf16[32,640]{1,0:T(8,128)(2,1)S(1)}, u32[]{:S(2)}, u32[]{:S(2)}) collective-permute-start(bf16[32,640]{1,0:T(8,128)(2,1)S(1)} %get-tuple-element.20), channel_id=1, source_target_pairs={{0,1},{1,0},{2,3},{3,2},{4,5},{5,4},{6,7},{7,6},{8,9},{9,8},{10,11... | collective-permute-start | bytes 122888 | tf_op jit(solution)/shard_map/ppermute | solution.py:208
